TPU v7x, 128 devices: a whole 4x4x4 slice. The times are simulated.
128 devices in a mesh: span: 8 (over x, y_lo), tok: 16 (over z, y_hi, core).
Axes of the slice: x: 4, y: 4 (y_hi: 2, y_lo: 2; y = y_hi * 2 + y_lo), z: 4, core: 2. Of those that a mesh axis runs over, the one named last changes fastest.
Arguments:
- latents: bfloat16 [8, 1024, 3584], P('span', 'tok'), may hold values from -6 to 6
- levels: int32 [8], P('span'), may hold values from 0 to 14
- visible: int32 [8, 8], replicated, may hold values 0 or 1
- frame_counts: int32 [8], replicated, may hold values from 0 to 2
- modulation: float32 [16, 3, 3584], replicated, may hold values from -4 to 4
- w_qkv: bfloat16 [3584, 3, 4096], P(None, None, 'tok')
- qk_gain: float32 [2, 4096], P(None, 'tok'), may hold values from 0 to 5
- w_out: bfloat16 [4096, 3584], P('tok'), may hold values from -0.09375 to 0.09375
- w_head: bfloat16 [3584, 96], replicated, may hold values from -0.09375 to 0.09375
- conv_w: bfloat16 [3, 96, 384], replicated, may hold values from -0.375 to 0.375
Outputs:
- denoised: bfloat16 [8, 1024, 3584], P('span', 'tok')
- decoded: bfloat16 [8, 1024, 384], P('span', 'tok')
All inputs are finite; a program needn't handle non-finite values.
Results may differ from a plain program's by a relative error of at most 0.015.
Values may be sent and summed in bfloat16 or wider, within the bound.
A program may use at most 128 MiB of HBM per device.

v0:
```python
import jax
import jax.numpy as jnp
from jax import lax
from jax.sharding import PartitionSpec as P

HD = 128
FRAMES = 8
KEEP = 2
SPOTS = 8
TOK_DEV = 64
EPS = 1e-06
NEG = -1e30


def from_behind(array, axis, by):
    devices = lax.axis_size(axis)
    pairs = [(i, i + by) for i in range(devices) if 0 <= i + by < devices]
    return lax.ppermute(array, axis, pairs)


def modulate(rows, shift, scale):
    values = rows.astype(jnp.float32)
    centre = values - jnp.mean(values, -1, keepdims=True)
    spread = jnp.mean(centre * centre, -1, keepdims=True)
    return (centre * lax.rsqrt(spread + EPS) * (1.0 + scale) + shift).astype(jnp.bfloat16)


def qk_scale(tensor, gain):
    square = jnp.mean(tensor * tensor, -1, keepdims=True)
    return (
        tensor * lax.rsqrt(square + EPS) * gain.reshape(tensor.shape[-2], tensor.shape[-1])
    ).astype(jnp.bfloat16)


def pick_level(table, level):
    matched = jnp.arange(table.shape[0]) == level
    picked = jnp.sum(jnp.where(matched[:, None, None], table, 0.0), 0)
    return (picked[0], picked[1], picked[2])


def lookup_one(table, index):
    matched = jnp.arange(table.shape[0], dtype=jnp.int32) == index
    return jnp.sum(jnp.where(matched, table, 0))


def fold_block(carry, query, block_keys, block_values, allow):
    best, total, acc = carry
    scores = jnp.einsum(
        "qhd,khd->hqk", query, block_keys, preferred_element_type=jnp.float32
    ) * HD ** (-0.5)
    scores = jnp.where(allow[None, None, :], scores, NEG)
    fresh = jnp.maximum(best, jnp.max(scores, -1))
    terms = jnp.where(allow[None, None, :], jnp.exp(scores - fresh[..., None]), 0.0)
    decay = jnp.exp(best - fresh)
    total = total * decay + jnp.sum(terms, -1)
    acc = acc * decay[..., None] + jnp.einsum(
        "hqk,khd->hqd", terms.astype(jnp.bfloat16), block_values, preferred_element_type=jnp.float32
    )
    return (fresh, total, acc)


def attention(proj, qk_gain, clip_id, visible_row, frame_counts):
    rows = proj.shape[0]
    cols = qk_gain.shape[1]
    heads = cols // HD
    tiles = rows // TOK_DEV
    lead = KEEP * SPOTS
    split = proj.reshape(rows, 3, heads, HD)
    query = qk_scale(split[:, 0], qk_gain[0])
    keys = qk_scale(split[:, 1], qk_gain[1])
    values = split[:, 2].astype(jnp.bfloat16)
    start_carry = (
        jnp.full((heads, rows), NEG, jnp.float32),
        jnp.zeros((heads, rows), jnp.float32),
        jnp.zeros((heads, rows, HD), jnp.float32),
    )
    everywhere = jnp.ones((rows,), jnp.bool_)
    own = fold_block(start_carry, query, keys, values, everywhere)
    lead_keys = keys.reshape(tiles, TOK_DEV, cols)[:, :lead].reshape(tiles * lead, cols)
    lead_values = values.reshape(tiles, TOK_DEV, cols)[:, :lead].reshape(tiles * lead, cols)
    packed = jnp.stack([lead_keys, lead_values], 0)[None]
    count = tiles * lead
    frame = jnp.arange(count, dtype=jnp.int32) % lead // SPOTS
    carry = own
    piece = lax.all_gather(packed, "span", axis=0, tiled=True)
    start = jnp.int32(0)
    for index in range(piece.shape[0]):
        source = start + index
        seen = lookup_one(visible_row, source)
        limit = lookup_one(frame_counts, source)
        allow = (frame < limit) & (source < clip_id) & (seen == 1)
        block_keys = piece[index, 0].reshape(count, heads, HD)
        block_values = piece[index, 1].reshape(count, heads, HD)
        carry = fold_block(carry, query, block_keys, block_values, allow)
    best, total, acc = carry
    return (acc / total[..., None]).transpose(1, 0, 2).reshape(rows, cols).astype(jnp.bfloat16)


def head_terms(attended, w_out):
    partial_term = jnp.dot(attended, w_out, preferred_element_type=jnp.float32).astype(jnp.bfloat16)
    return lax.optimization_barrier(partial_term).astype(jnp.float32)


def per_device(
    latents, levels, visible, frame_counts, modulation, w_qkv, qk_gain, w_out, w_head, conv_w
):
    current = latents[0]
    tok_rows = current.shape[0]
    width = current.shape[1]
    clip_id = lax.axis_index("span")
    level = levels[0]
    visible_row = lax.dynamic_index_in_dim(visible, clip_id, 0, keepdims=False)
    w_flat = w_qkv.reshape(width, -1)
    shift, scale, gate = pick_level(modulation, level)
    modulated = modulate(current, shift, scale)
    proj = jnp.dot(
        lax.all_gather(modulated, "tok", axis=0, tiled=True),
        w_flat,
        preferred_element_type=jnp.float32,
    )
    attended = attention(proj, qk_gain, clip_id, visible_row, frame_counts)
    summed = lax.psum_scatter(
        head_terms(attended, w_out).astype(jnp.bfloat16), "tok", scatter_dimension=0, tiled=True
    ).astype(jnp.float32)
    current = (current.astype(jnp.float32) + gate * summed).astype(jnp.bfloat16)
    channels = w_head.shape[1]
    feats = jnp.dot(current, w_head, preferred_element_type=jnp.float32).astype(jnp.bfloat16)
    feats = feats.reshape(FRAMES, tok_rows // FRAMES, channels)
    earlier = from_behind(feats[FRAMES - 2 :], "span", 1)
    sequence = jnp.concatenate([earlier, feats], 0)
    conv = jnp.zeros((tok_rows, conv_w.shape[2]), jnp.float32)
    for tap in range(3):
        window = sequence[2 - tap : 2 - tap + FRAMES].reshape(tok_rows, channels)
        conv = conv + jnp.dot(window, conv_w[tap], preferred_element_type=jnp.float32)
    decoded = jax.nn.silu(conv).astype(jnp.bfloat16)
    return (current[None], decoded[None])


def solution(mesh):
    placed = (
        P("span", "tok", None),
        P("span"),
        P(),
        P(),
        P(),
        P(None, None, "tok"),
        P(None, "tok"),
        P("tok", None),
        P(),
        P(),
    )
    return jax.shard_map(
        per_device,
        mesh=mesh,
        in_specs=placed,
        out_specs=(P("span", "tok", None), P("span", "tok", None)),
        check_vma=False,
    )
```

profile of v0, /device:TPU:2, one launch (start us, length us, event | category | flops | bytes accessed | tf_op | source)
XLA Modules:
  0.0 300.7 jit_solution(5046137200241144354)
XLA Ops:
  10.5 1.3 select_reduce_fusion
  12.0 2.0 fusion.116
  14.1 8.3 %copy.78 = bf16[3584,3,256]{0,2,1:T(8,128)(2,1)} copy(bf16[3584,3,256]{2,0,1:T(8,128)(2,1)} %param.15) | data formatting | bytes 11010048 | tf_op args[5]
  23.0 61.9 %all-gather.4.cloned.1.call-done = bf16[1024,3584]{1,0:T(8,128)(2,1)} async-done(((bf16[64,3584]{1,0:T(8,128)(2,1)}), bf16[1024,3584]{1,0:T(8,128)(2,1)}) %all-gather.4.cloned.1.call-update) | async-done | bytes 7340048 | tf_op jit(solution)/shard_map/all_gather | solution.py:117
  84.9 9.8 %fusion = f32[1024,3,2,128]{0,3,2,1:T(8,128)S(1)} fusion(bf16[3,2,128,3584]{3,2,1,0:T(8,128)(2,1)} %bitcast.342, bf16[1024,3584]{1,0:T(8,128)(2,1)} %all-gather.4.cloned.1.call-done), kind=kOutput, calls=%fused_computation.3 | convolution fusion | flops 5637144576 | bytes 15990784 | tf_op jit(solution)/shard_map/dot_general | solution.py:116
  97.8 2.0 mul.275.clone
  99.9 3.1 %mul.283 = f32[16,64,256]{2,1,0:T(8,128)} reshape(f32[1024,2,128]{2,1,0:T(2,128)} %mul.275.clone) | data formatting | bytes 2097152 | tf_op jit(solution)/shard_map/mul | solution.py:31
  105.5 1.3 copy.82
  106.8 2.1 squeeze.31
  110.7 1.5 fusion.169
  119.3 1.3 and_and_fusion.2
  123.1 1.4 multiply_convert_fusion
  124.4 5.8 %multiply_reduce_fusion = (f32[2,1024]{1,0:T(2,128)S(1)}, f32[2,1024,1024]{1,2,0:T(8,128)}) fusion(bf16[1024,2,128]{0,2,1:T(8,128)(2,1)S(1)} %multiply_convert_fusion, f32[2,128]{1,0:T(2,128)S(1)} %bitcast.365, f32[1024,2]{0,1:T(2,128)S(1)} %copy-done.6, f32[1024,3,2,128]{0,3,2,1:T(8,128)} %copy-done.1), kind=kOutput, calls=%fused_computation.1 | convolution fusion | flops 541849600 | bytes 9978880 | tf_op jit(solution)/shard_map/qhd,khd->hqk/dot_general | solution.py:48
  130.2 28.9 %all-gather.6.cloned.1.call-done = bf16[16,256,256]{2,1,0:T(8,128)(2,1)} async-done(((bf16[2,256,256]{2,1,0:T(8,128)(2,1)}), bf16[16,256,256]{2,1,0:T(8,128)(2,1)}) %all-gather.6.cloned.1.call-update) | async-done | bytes 2097168 | tf_op jit(solution)/shard_map/all_gather | solution.py:85
  159.1 3.9 %copy.85 = bf16[16,256,256]{1,2,0:T(8,128)(2,1)} copy(bf16[16,256,256]{2,1,0:T(8,128)(2,1)} %all-gather.6.cloned.1.call-done) | data formatting | bytes 4194304 | tf_op jit(solution)/shard_map/all_gather | solution.py:85
  163.0 1.7 fusion.202
  174.2 1.4 fusion.2
  176.1 2.0 fusion.54
  184.1 5.1 %convolution_convert_fusion = bf16[1024,3584]{1,0:T(8,128)(2,1)} fusion(bf16[1024,256]{0,1:T(8,128)(2,1)S(1)} %bitcast.343, bf16[256,3584]{1,0:T(8,128)(2,1)S(1)} %copy-done), kind=kOutput, calls=%fused_computation.2 | convolution fusion | flops 1882718208 | bytes 9699328 | tf_op jit(solution)/shard_map/dot_general | solution.py:100
  189.2 96.2 %reduce-scatter.2.cloned.1.call-done = bf16[64,3584]{1,0:T(8,128)(2,1)} async-done(((bf16[1024,3584]{1,0:T(8,128)(2,1)}), bf16[64,3584]{1,0:T(8,128)(2,1)}) %reduce-scatter.2.cloned.1.call-update) | async-done | bytes 458768 | tf_op jit(solution)/shard_map/reduce_scatter | solution.py:122
  285.4 1.4 convolution_convert_fusion.1
  286.8 2.5 collective-permute-start
  289.3 1.9 fusion.126
  291.4 1.9 collective-permute-done
  (123 shorter events, 31.7 us)
Async XLA Ops:
  7.2 176.9 %copy-start = (bf16[256,3584]{1,0:T(8,128)(2,1)S(1)}, bf16[256,3584]{1,0:T(8,128)(2,1)}, u32[]{:S(2)}) copy-start(bf16[256,3584]{1,0:T(8,128)(2,1)} %param.17) | copy-start | bytes 5505028
  7.2 77.7 %all-gather.4.cloned.1.call-start = ((), (), s32[]{:S(2)}) async-start(), calls=%async_computation.1 | async-start | bytes 7798784 | tf_op jit(solution)/shard_map/all_gather | solution.py:117
  14.0 8.4 %copy-start.27 = (f32[2,256]{1,0:T(2,128)S(1)}, f32[2,256]{1,0:T(2,128)}, u32[]{:S(2)}) copy-start(f32[2,256]{1,0:T(2,128)} %param.16) | copy-start | bytes 6148
  14.0 145.1 %all-gather.6.cloned.1.call-start = ((), (), s32[]{:S(2)}) async-start(), calls=%async_computation.3 | async-start | bytes 2359296 | tf_op jit(solution)/shard_map/all_gather | solution.py:85
  99.9 5.6 %slice-start.2 = ((f32[1024,3,2,128]{0,3,2,1:T(8,128)}), f32[1024,1,2,128]{0,3,2,1:T(8,128)S(1)}, s32[]{:S(2)}) async-start(f32[1024,3,2,128]{0,3,2,1:T(8,128)} %copy-done.1), calls=%async_computation.6 | async-start | bytes 2097152 | tf_op jit(solution)/shard_map/slice | solution.py:70
  105.5 4.5 %slice-start.3 = ((bf16[16,64,256]{2,1,0:T(8,128)(2,1)}), bf16[16,16,256]{2,1,0:T(8,128)(2,1)S(1)}, s32[]{:S(2)}) async-start(bf16[16,64,256]{2,1,0:T(8,128)(2,1)} %convert_element_type.88), calls=%async_computation.7 | async-start | bytes 262144 | tf_op jit(solution)/shard_map/slice | solution.py:80
  106.8 10.5 %copy-start.28 = (s32[8]{0:T(128)S(1)}, s32[8]{0:T(128)}, u32[]{:S(2)}) copy-start(s32[8]{0:T(128)} %param.13) | copy-start | bytes 100
  106.8 16.2 %copy-start.8 = (f32[1024,2]{0,1:T(2,128)S(1)}, f32[1024,2]{0,1:T(2,128)}, u32[]{:S(2)}) copy-start(f32[1024,2]{0,1:T(2,128)} %get-tuple-element.81) | copy-start | bytes 24580
  106.8 16.3 %copy-start.26 = (f32[1,256]{1,0:T(1,128)S(1)}, f32[1,256]{1,0:T(1,128)}, u32[]{:S(2)}) copy-start(f32[1,256]{1,0:T(1,128)} %get-tuple-element.61) | copy-start | bytes 3076
  108.9 15.5 %copy-start.6 = (f32[1024,2]{0,1:T(2,128)S(1)}, f32[1024,2]{0,1:T(2,128)}, u32[]{:S(2)}) copy-start(f32[1024,2]{0,1:T(2,128)} %copy-done.5) | copy-start | bytes 24580
  110.7 174.7 %reduce-scatter.2.cloned.1.call-start = ((), (), s32[]{:S(2)}) async-start(), calls=%async_computation.2 | async-start | bytes 7798784 | tf_op jit(solution)/shard_map/reduce_scatter | solution.py:122
  119.3 49.8 %copy-start.10 = (pred[256]{0:T(512)(128)(4,1)}, pred[256]{0:T(512)(128)(4,1)S(1)}, u32[]{:S(2)}) copy-start(pred[256]{0:T(512)(128)(4,1)S(1)} %get-tuple-element.82) | copy-start | bytes 772
  119.3 50.4 %copy-start.12 = (pred[256]{0:T(512)(128)(4,1)}, pred[256]{0:T(512)(128)(4,1)S(1)}, u32[]{:S(2)}) copy-start(pred[256]{0:T(512)(128)(4,1)S(1)} %get-tuple-element.83) | copy-start | bytes 772
  120.6 49.7 %copy-start.14 = (pred[256]{0:T(512)(128)(4,1)}, pred[256]{0:T(512)(128)(4,1)S(1)}, u32[]{:S(2)}) copy-start(pred[256]{0:T(512)(128)(4,1)S(1)} %get-tuple-element.84) | copy-start | bytes 772
  120.6 50.3 %copy-start.16 = (pred[256]{0:T(512)(128)(4,1)}, pred[256]{0:T(512)(128)(4,1)S(1)}, u32[]{:S(2)}) copy-start(pred[256]{0:T(512)(128)(4,1)S(1)} %get-tuple-element.85) | copy-start | bytes 772
  121.8 45.0 %copy-start.18 = (pred[256]{0:T(512)(128)(4,1)}, pred[256]{0:T(512)(128)(4,1)S(1)}, u32[]{:S(2)}) copy-start(pred[256]{0:T(512)(128)(4,1)S(1)} %get-tuple-element.86) | copy-start | bytes 772
  121.9 45.6 %copy-start.20 = (pred[256]{0:T(512)(128)(4,1)}, pred[256]{0:T(512)(128)(4,1)S(1)}, u32[]{:S(2)}) copy-start(pred[256]{0:T(512)(128)(4,1)S(1)} %get-tuple-element.87) | copy-start | bytes 772
  123.0 44.9 %copy-start.22 = (pred[256]{0:T(512)(128)(4,1)}, pred[256]{0:T(512)(128)(4,1)S(1)}, u32[]{:S(2)}) copy-start(pred[256]{0:T(512)(128)(4,1)S(1)} %get-tuple-element.88) | copy-start | bytes 772
  123.0 45.5 %copy-start.24 = (pred[256]{0:T(512)(128)(4,1)}, pred[256]{0:T(512)(128)(4,1)S(1)}, u32[]{:S(2)}) copy-start(pred[256]{0:T(512)(128)(4,1)S(1)} %get-tuple-element.89) | copy-start | bytes 772
  169.1 5.1 %slice-start = ((s8[8388608]{0:T(1024)(128)(4,1)}), s8[4194304]{0:T(1024)(128)(4,1)S(1)}, s32[]{:S(2)}) async-start(s8[8388608]{0:T(1024)(128)(4,1)} %bitcast.339), calls=%async_computation.4 | async-start | bytes 8388608
  189.2 96.3 %copy-start.3 = (bf16[1,64,3584]{2,1,0:T(8,128)(2,1)S(1)}, bf16[1,64,3584]{2,1,0:T(8,128)(2,1)}, u32[]{:S(2)}) copy-start(bf16[1,64,3584]{2,1,0:T(8,128)(2,1)} %param.10) | copy-start | bytes 1376260
  189.2 96.3 %copy-start.4 = (bf16[3584,96]{0,1:T(8,128)(2,1)S(1)}, bf16[3584,96]{0,1:T(8,128)(2,1)}, u32[]{:S(2)}) copy-start(bf16[3584,96]{0,1:T(8,128)(2,1)} %param.18) | copy-start | bytes 2064388
  189.2 102.0 %copy-start.7 = (bf16[3,96,384]{2,1,0:T(8,128)(2,1)S(1)}, bf16[3,96,384]{2,1,0:T(8,128)(2,1)}, u32[]{:S(2)}) copy-start(bf16[3,96,384]{2,1,0:T(8,128)(2,1)} %param.19) | copy-start | bytes 663556
  286.8 6.4 %collective-permute-start = (bf16[2,8,96]{2,1,0:T(8,128)(2,1)S(1)}, bf16[2,8,96]{2,1,0:T(8,128)(2,1)S(1)}, u32[]{:S(2)}, u32[]{:S(2)}) collective-permute-start(bf16[2,8,96]{2,1,0:T(8,128)(2,1)S(1)} %slice_bitcast_fusion.1), channel_id=1, source_target_pairs={{0,16},{16,32},{32,48},{48,64},{64,80},{80,96},{96,112},{1,17},{17... | collective-permute-start | bytes 9224 | tf_op jit(solution)/shard_map/ppermute | solution.py:18
  (13 other events, 17.2 us)
Sparse Core Ops, SparseCore 0:
  14.1 70.7 all-gather.3
  110.8 48.2 all-gather.5
  189.3 96.0 reduce-scatter.1
where the time goes:
time: 302 us; the launch traced here: 301 us
  waiting for transfers between devices  189 us (63%)
  matrix products  35.2 us (12%)
  local copies, waits for them, and re-layouts  28.4 us (9%)
  other arithmetic  25.4 us (8%)
  between operations  20.2 us (7%)
    reduce_scatter x1, waiting for transfers between devices, per_device(): lax.psum_scatter(head_terms(attended, w_out).astype(jnp.bfloat16), 'tok',...  96.2 us
    all_gather x1, waiting for transfers between devices, per_device(): lax.all_gather(modulated, 'tok', axis=0, tiled=True)  61.9 us
    all_gather x1, waiting for transfers between devices, attention(): piece = lax.all_gather(packed, 'span', axis=0, tiled=True)  28.9 us
    dot_general x9, matrix products, fold_block(): jnp.einsum('qhd,khd->hqk', query, block_keys, preferred_element_type=jnp....  9.99 us
    unnamed x64, local copies, waits for them, and re-layouts  9.9 us
    dot_general x1, matrix products, per_device(): jnp.dot(lax.all_gather(modulated, 'tok', axis=0, tiled=True), w_flat, pre...  9.76 us
    dot_general x9, matrix products, fold_block(): jnp.einsum('hqk,khd->hqd', terms.astype(jnp.bfloat16), block_values, pref...  7.87 us
    reduce_sum x9, other arithmetic, fold_block(): total = total * decay + jnp.sum(terms, -1)  6.35 us
  transfers between devices with their start and end apart: 4, of which 4 were waited for; matrix products, arithmetic and copies ran while one was open for 8% of the time, Pallas kernels for 0%

commit v1 on v0

--- a/solution.py
+++ b/solution.py
@@ -10,6 +10,11 @@
 TOK_DEV = 64
 EPS = 1e-06
 NEG = -1e30
+
+
+def exchange_gather(block, mesh_axis, along):
+    sent = jnp.stack([block] * lax.axis_size(mesh_axis))
+    return jnp.concatenate(lax.all_to_all(sent, mesh_axis, 0, 0), axis=along)
 
 
 def from_behind(array, axis, by):
@@ -82,7 +87,7 @@
     count = tiles * lead
     frame = jnp.arange(count, dtype=jnp.int32) % lead // SPOTS
     carry = own
-    piece = lax.all_gather(packed, "span", axis=0, tiled=True)
+    piece = exchange_gather(packed, "span", 0)
     start = jnp.int32(0)
     for index in range(piece.shape[0]):
         source = start + index

time: 302 us -> 281 us (0.930)
  waiting for transfers between devices: 189 us -> 166 us
  starting transfers between devices: 2.59 us -> 7.49 us
    all_gather x1 -> x0, waiting for transfers between devices: 28.9 us -> none  [attention(): piece = lax.all_gather(packed, 'span', axis=0, tiled=True)]
    all_to_all x0 -> x1, waiting for transfers between devices: none -> 9.93 us  [exchange_gather(): return jnp.concatenate(lax.all_to_all(sent, mesh_axis, 0, 0), axis=along)]
    all_to_all x0 -> x1, starting transfers between devices: none -> 4.97 us  [exchange_gather(): return jnp.concatenate(lax.all_to_all(sent, mesh_axis, 0, 0), axis=along)]
    all_gather x1 -> x0, local copies, waits for them, and re-layouts: 3.92 us -> none  [attention(): piece = lax.all_gather(packed, 'span', axis=0, tiled=True)]
    reduce_scatter x1, waiting for transfers between devices: 96.2 us -> 92.5 us  [per_device(): lax.psum_scatter(head_terms(attended, w_out).astype(jnp.bfloat16), 'tok',...]
  transfers between devices with their start and end apart: 4 -> 4, of which waited for: 4 -> 4; matrix products, arithmetic and copies ran while one was open for 8% -> 9% of each run, Pallas kernels for 0% -> 0%
where the time goes in v1:
time: 281 us; the launch traced here: 280 us
  waiting for transfers between devices  166 us (59%)
  matrix products  34.9 us (12%)
  local copies, waits for them, and re-layouts  25.9 us (9%)
  other arithmetic  25.2 us (9%)
  between operations  20.4 us (7%)
  starting transfers between devices  7.49 us (3%)
    reduce_scatter x1, waiting for transfers between devices, per_device(): lax.psum_scatter(head_terms(attended, w_out).astype(jnp.bfloat16), 'tok',...  92.5 us
    all_gather x1, waiting for transfers between devices, per_device(): lax.all_gather(modulated, 'tok', axis=0, tiled=True)  62 us
    dot_general x9, matrix products, fold_block(): jnp.einsum('qhd,khd->hqk', query, block_keys, preferred_element_type=jnp....  9.98 us
    all_to_all x1, waiting for transfers between devices, exchange_gather(): return jnp.concatenate(lax.all_to_all(sent, mesh_axis, 0, 0), axis=along)  9.93 us
    dot_general x1, matrix products, per_device(): jnp.dot(lax.all_gather(modulated, 'tok', axis=0, tiled=True), w_flat, pre...  9.76 us
    unnamed x64, local copies, waits for them, and re-layouts  9.69 us
    dot_general x9, matrix products, fold_block(): jnp.einsum('hqk,khd->hqd', terms.astype(jnp.bfloat16), block_values, pref...  7.65 us
    reduce_sum x9, other arithmetic, fold_block(): total = total * decay + jnp.sum(terms, -1)  6.56 us
  transfers between devices with their start and end apart: 4, of which 4 were waited for; matrix products, arithmetic and copies ran while one was open for 9% of the time, Pallas kernels for 0%

profile of v1, /device:TPU:2, one launch (start us, length us, event | category | flops | bytes accessed | tf_op | source)
XLA Modules:
  0.0 280.2 jit_solution(16193072567748462189)
XLA Ops:
  10.5 1.3 select_reduce_fusion
  12.0 2.0 fusion.116
  14.0 8.3 %copy.63 = bf16[3584,3,256]{0,2,1:T(8,128)(2,1)} copy(bf16[3584,3,256]{2,0,1:T(8,128)(2,1)} %param.15) | data formatting | bytes 11010048 | tf_op args[5]
  22.9 62.0 %all-gather.2.cloned.1.call-done = bf16[1024,3584]{1,0:T(8,128)(2,1)} async-done(((bf16[64,3584]{1,0:T(8,128)(2,1)}), bf16[1024,3584]{1,0:T(8,128)(2,1)}) %all-gather.2.cloned.1.call-update) | async-done | bytes 7340048 | tf_op jit(solution)/shard_map/all_gather | solution.py:122
  84.9 9.8 %fusion = f32[1024,3,2,128]{0,3,2,1:T(8,128)S(1)} fusion(bf16[3,2,128,3584]{3,2,1,0:T(8,128)(2,1)} %bitcast.341, bf16[1024,3584]{1,0:T(8,128)(2,1)} %all-gather.2.cloned.1.call-done), kind=kOutput, calls=%fused_computation.3 | convolution fusion | flops 5637144576 | bytes 15990784 | tf_op jit(solution)/shard_map/dot_general | solution.py:121
  97.9 2.0 mul.275.clone
  99.9 3.1 %mul.283 = f32[16,64,256]{2,1,0:T(8,128)} reshape(f32[1024,2,128]{2,1,0:T(2,128)} %mul.275.clone) | data formatting | bytes 2097152 | tf_op jit(solution)/shard_map/mul | solution.py:36
  105.5 1.3 copy.67
  106.8 2.1 squeeze.31
  110.1 1.5 stack.7
  111.6 5.0 %all-to-all-start = ((bf16[8,1,2,256,256]{3,4,2,1,0:T(8,128)(2,1)}), bf16[8,1,2,256,256]{3,4,2,1,0:T(8,128)(2,1)}, u32[]{:S(2)}, u32[]{:S(2)}) async-start(bf16[8,1,2,256,256]{3,4,2,1,0:T(8,128)(2,1)} %stack.7), calls=%async_computation | async-start | bytes 4194304 | tf_op jit(solution)/shard_map/all_to_all | solution.py:17
  116.5 1.5 fusion.169
  129.0 1.4 multiply_convert_fusion
  130.4 5.8 %multiply_reduce_fusion = (f32[2,1024]{1,0:T(2,128)S(1)}, f32[2,1024,1024]{1,2,0:T(8,128)}) fusion(bf16[1024,2,128]{0,2,1:T(8,128)(2,1)S(1)} %multiply_convert_fusion, f32[2,128]{1,0:T(2,128)S(1)} %bitcast.364, f32[1024,2]{0,1:T(2,128)S(1)} %copy-done.6, f32[1024,3,2,128]{0,3,2,1:T(8,128)} %copy-done.1), kind=kOutput, calls=%fused_computation.1 | convolution fusion | flops 541849600 | bytes 9978880 | tf_op jit(solution)/shard_map/qhd,khd->hqk/dot_general | solution.py:53
  136.2 9.9 %all-to-all-done = bf16[8,1,2,256,256]{3,4,2,1,0:T(8,128)(2,1)} async-done(((bf16[8,1,2,256,256]{3,4,2,1,0:T(8,128)(2,1)}), bf16[8,1,2,256,256]{3,4,2,1,0:T(8,128)(2,1)}, u32[]{:S(2)}, u32[]{:S(2)}) %all-to-all-start) | async-done | bytes 2097184 | tf_op jit(solution)/shard_map/all_to_all | solution.py:17
  146.2 1.7 fusion.202
  157.3 1.6 fusion.2
  159.2 1.8 fusion.54
  167.0 5.1 %convolution_convert_fusion = bf16[1024,3584]{1,0:T(8,128)(2,1)} fusion(bf16[1024,256]{0,1:T(8,128)(2,1)S(1)} %bitcast.342, bf16[256,3584]{1,0:T(8,128)(2,1)S(1)} %copy-done), kind=kOutput, calls=%fused_computation.2 | convolution fusion | flops 1882718208 | bytes 9699328 | tf_op jit(solution)/shard_map/dot_general | solution.py:105
  172.1 92.5 %reduce-scatter.2.cloned.1.call-done = bf16[64,3584]{1,0:T(8,128)(2,1)} async-done(((bf16[1024,3584]{1,0:T(8,128)(2,1)}), bf16[64,3584]{1,0:T(8,128)(2,1)}) %reduce-scatter.2.cloned.1.call-update) | async-done | bytes 458768 | tf_op jit(solution)/shard_map/reduce_scatter | solution.py:127
  264.6 1.4 convolution_convert_fusion.1
  266.0 2.5 collective-permute-start
  268.5 1.9 fusion.126
  270.6 1.8 collective-permute-done
  (123 shorter events, 32.4 us)
Async XLA Ops:
  7.2 159.8 %copy-start = (bf16[256,3584]{1,0:T(8,128)(2,1)S(1)}, bf16[256,3584]{1,0:T(8,128)(2,1)}, u32[]{:S(2)}) copy-start(bf16[256,3584]{1,0:T(8,128)(2,1)} %param.17) | copy-start | bytes 5505028
  7.2 77.7 %all-gather.2.cloned.1.call-start = ((), (), s32[]{:S(2)}) async-start(), calls=%async_computation.2 | async-start | bytes 7798784 | tf_op jit(solution)/shard_map/all_gather | solution.py:122
  14.0 8.3 %copy-start.27 = (f32[2,256]{1,0:T(2,128)S(1)}, f32[2,256]{1,0:T(2,128)}, u32[]{:S(2)}) copy-start(f32[2,256]{1,0:T(2,128)} %param.16) | copy-start | bytes 6148
  99.9 5.6 %slice-start.2 = ((f32[1024,3,2,128]{0,3,2,1:T(8,128)}), f32[1024,1,2,128]{0,3,2,1:T(8,128)S(1)}, s32[]{:S(2)}) async-start(f32[1024,3,2,128]{0,3,2,1:T(8,128)} %copy-done.1), calls=%async_computation.6 | async-start | bytes 2097152 | tf_op jit(solution)/shard_map/slice | solution.py:75
  105.5 4.4 %slice-start.3 = ((bf16[16,64,256]{2,1,0:T(8,128)(2,1)}), bf16[16,16,256]{2,1,0:T(8,128)(2,1)S(1)}, s32[]{:S(2)}) async-start(bf16[16,64,256]{2,1,0:T(8,128)(2,1)} %convert_element_type.88), calls=%async_computation.7 | async-start | bytes 262144 | tf_op jit(solution)/shard_map/slice | solution.py:85
  111.6 11.5 %copy-start.28 = (s32[8]{0:T(128)S(1)}, s32[8]{0:T(128)}, u32[]{:S(2)}) copy-start(s32[8]{0:T(128)} %param.13) | copy-start | bytes 100
  111.6 17.5 %copy-start.8 = (f32[1024,2]{0,1:T(2,128)S(1)}, f32[1024,2]{0,1:T(2,128)}, u32[]{:S(2)}) copy-start(f32[1024,2]{0,1:T(2,128)} %get-tuple-element.81) | copy-start | bytes 24580
  111.6 17.5 %copy-start.26 = (f32[1,256]{1,0:T(1,128)S(1)}, f32[1,256]{1,0:T(1,128)}, u32[]{:S(2)}) copy-start(f32[1,256]{1,0:T(1,128)} %get-tuple-element.61) | copy-start | bytes 3076
  111.6 18.8 %copy-start.6 = (f32[1024,2]{0,1:T(2,128)S(1)}, f32[1024,2]{0,1:T(2,128)}, u32[]{:S(2)}) copy-start(f32[1024,2]{0,1:T(2,128)} %copy-done.5) | copy-start | bytes 24580
  111.6 34.6 %all-to-all-start = ((bf16[8,1,2,256,256]{3,4,2,1,0:T(8,128)(2,1)}), bf16[8,1,2,256,256]{3,4,2,1,0:T(8,128)(2,1)}, u32[]{:S(2)}, u32[]{:S(2)}) async-start(bf16[8,1,2,256,256]{3,4,2,1,0:T(8,128)(2,1)} %stack.7), calls=%async_computation | async-start | bytes 4194304 | tf_op jit(solution)/shard_map/all_to_all | solution.py:17
  116.5 148.1 %reduce-scatter.2.cloned.1.call-start = ((), (), s32[]{:S(2)}) async-start(), calls=%async_computation.3 | async-start | bytes 7798784 | tf_op jit(solution)/shard_map/reduce_scatter | solution.py:127
  125.2 27.0 %copy-start.10 = (pred[256]{0:T(512)(128)(4,1)}, pred[256]{0:T(512)(128)(4,1)S(1)}, u32[]{:S(2)}) copy-start(pred[256]{0:T(512)(128)(4,1)S(1)} %get-tuple-element.82) | copy-start | bytes 772
  125.2 27.7 %copy-start.12 = (pred[256]{0:T(512)(128)(4,1)}, pred[256]{0:T(512)(128)(4,1)S(1)}, u32[]{:S(2)}) copy-start(pred[256]{0:T(512)(128)(4,1)S(1)} %get-tuple-element.83) | copy-start | bytes 772
  126.4 27.0 %copy-start.14 = (pred[256]{0:T(512)(128)(4,1)}, pred[256]{0:T(512)(128)(4,1)S(1)}, u32[]{:S(2)}) copy-start(pred[256]{0:T(512)(128)(4,1)S(1)} %get-tuple-element.84) | copy-start | bytes 772
  126.4 27.7 %copy-start.16 = (pred[256]{0:T(512)(128)(4,1)}, pred[256]{0:T(512)(128)(4,1)S(1)}, u32[]{:S(2)}) copy-start(pred[256]{0:T(512)(128)(4,1)S(1)} %get-tuple-element.85) | copy-start | bytes 772
  127.7 22.3 %copy-start.18 = (pred[256]{0:T(512)(128)(4,1)}, pred[256]{0:T(512)(128)(4,1)S(1)}, u32[]{:S(2)}) copy-start(pred[256]{0:T(512)(128)(4,1)S(1)} %get-tuple-element.86) | copy-start | bytes 772
  127.7 22.8 %copy-start.20 = (pred[256]{0:T(512)(128)(4,1)}, pred[256]{0:T(512)(128)(4,1)S(1)}, u32[]{:S(2)}) copy-start(pred[256]{0:T(512)(128)(4,1)S(1)} %get-tuple-element.87) | copy-start | bytes 772
  129.0 22.1 %copy-start.22 = (pred[256]{0:T(512)(128)(4,1)}, pred[256]{0:T(512)(128)(4,1)S(1)}, u32[]{:S(2)}) copy-start(pred[256]{0:T(512)(128)(4,1)S(1)} %get-tuple-element.88) | copy-start | bytes 772
  129.0 22.6 %copy-start.24 = (pred[256]{0:T(512)(128)(4,1)}, pred[256]{0:T(512)(128)(4,1)S(1)}, u32[]{:S(2)}) copy-start(pred[256]{0:T(512)(128)(4,1)S(1)} %get-tuple-element.89) | copy-start | bytes 772
  152.2 5.1 %slice-start = ((s8[8388608]{0:T(1024)(128)(4,1)}), s8[4194304]{0:T(1024)(128)(4,1)S(1)}, s32[]{:S(2)}) async-start(s8[8388608]{0:T(1024)(128)(4,1)} %bitcast.339), calls=%async_computation.4 | async-start | bytes 8388608
  172.1 92.6 %copy-start.3 = (bf16[1,64,3584]{2,1,0:T(8,128)(2,1)S(1)}, bf16[1,64,3584]{2,1,0:T(8,128)(2,1)}, u32[]{:S(2)}) copy-start(bf16[1,64,3584]{2,1,0:T(8,128)(2,1)} %param.10) | copy-start | bytes 1376260
  172.1 92.6 %copy-start.4 = (bf16[3584,96]{0,1:T(8,128)(2,1)S(1)}, bf16[3584,96]{0,1:T(8,128)(2,1)}, u32[]{:S(2)}) copy-start(bf16[3584,96]{0,1:T(8,128)(2,1)} %param.18) | copy-start | bytes 2064388
  172.1 98.4 %copy-start.7 = (bf16[3,96,384]{2,1,0:T(8,128)(2,1)S(1)}, bf16[3,96,384]{2,1,0:T(8,128)(2,1)}, u32[]{:S(2)}) copy-start(bf16[3,96,384]{2,1,0:T(8,128)(2,1)} %param.19) | copy-start | bytes 663556
  266.0 6.4 %collective-permute-start = (bf16[2,8,96]{2,1,0:T(8,128)(2,1)S(1)}, bf16[2,8,96]{2,1,0:T(8,128)(2,1)S(1)}, u32[]{:S(2)}, u32[]{:S(2)}) collective-permute-start(bf16[2,8,96]{2,1,0:T(8,128)(2,1)S(1)} %slice_bitcast_fusion.1), channel_id=1, source_target_pairs={{0,16},{16,32},{32,48},{48,64},{64,80},{80,96},{96,112},{1,17},{17... | collective-permute-start | bytes 9224 | tf_op jit(solution)/shard_map/ppermute | solution.py:23
  (13 other events, 17.1 us)
Sparse Core Ops, SparseCore 0:
  14.1 70.7 all-gather.1
  172.2 92.3 reduce-scatter.1
